TPU v7x, 32 devices: a whole 2x2x4 slice. The times are simulated.
32 devices in a mesh: ctx: 8 (over z, core), inner: 4 (over y, x).
Axes of the slice: x: 2, y: 2, z: 4, core: 2. Of those that a mesh axis runs over, the one named last changes fastest.
Arguments:
- tokens: bfloat16 [4096, 2048], P(('ctx', 'inner')), may hold values from -6 to 6
- project_weight: bfloat16 [2048, 2, 4096], P('ctx', None, 'inner'), may hold values from -0.125 to 0.125
- state_weight: bfloat16 [2048, 2, 512], P('ctx', None, 'inner'), may hold values from -0.125 to 0.125
- step_weight: bfloat16 [2048, 64], P('ctx', 'inner'), may hold values from -0.125 to 0.125
- mixer_taps: float32 [5, 4096], P(None, 'inner'), may hold values from -2.5 to 2.5
- state_taps: float32 [5, 2, 512], replicated, may hold values from -2.5 to 2.5
- step_bias: float32 [64], P('inner'), may hold values from -4.6 to -2.3
- decay_log: float32 [64], P('inner'), may hold values from -13 to 0.5, as said below
- norm_gain: float32 [4096], replicated, may hold values from 0.1 to 1.9
Outputs:
- mixed_output: bfloat16 [4096, 4096], P(('ctx', 'inner'))
Inputs may be any that keep to these rules, and one draw needn't show every extreme that they name: `decay_log`: one value a head.
All inputs are finite; a program needn't handle non-finite values.
Results may differ from a plain program's by a relative error of at most 0.0075.
Values may be sent and summed in bfloat16 or wider, within the bound.
No kernel may reach another device: no remote copies, remote signals or barrier semaphores. Data moves between devices by JAX's collectives and lax.ppermute only.
A program may use at most 64 MiB of HBM per device.

v0:
```python
import jax
import jax.numpy as jnp
from jax import lax
from jax.sharding import PartitionSpec as P

H = 64
P_SIZE = 64
N = 128
G = 4
CONV = 4
SPAN = 128
EPSILON = 1e-05


def passed_along(x, axis, by):
    count = lax.axis_size(axis)
    pairs = [(i, i + by) for i in range(count) if 0 <= i + by < count]
    return lax.ppermute(x, axis, pairs)


def entering(x, axis, join, neutral):
    place = lax.axis_index(axis)
    gathered = jax.tree.map(
        lambda a, kind: lax.all_gather(a.astype(kind), axis), x, (jnp.bfloat16, jnp.bfloat16)
    )
    state = jax.tree.map(lambda a, e: jnp.zeros_like(a) + jnp.asarray(e, a.dtype), x, neutral)

    def one(turn, state):
        return join(
            state,
            jax.tree.map(
                lambda a, own: lax.dynamic_index_in_dim(a, turn, 0, False).astype(own.dtype),
                gathered,
                x,
            ),
        )

    return lax.fori_loop(0, place, one, state)


def partner(value, axis, stride):
    mask = 2**stride
    pairs = [(source, source ^ mask) for source in range(lax.axis_size(axis))]
    return lax.ppermute(value, axis, pairs)


def conv_apply(taps, previous, current):
    extended = jnp.concatenate([previous, current], axis=0)
    length_rows = current.shape[0]
    mixed = jnp.broadcast_to(taps[CONV], current.shape)
    for offset in range(CONV):
        mixed = mixed + taps[offset] * extended[offset : offset + length_rows].astype(jnp.float32)
    return jax.nn.silu(mixed).astype(jnp.bfloat16)


def join_chain(earlier, later):
    return (earlier[0] + later[0], jnp.exp(later[0])[:, None, None] * earlier[1] + later[1])


def carry_block(state, inputs):
    decay_sum, added = inputs
    return (jnp.exp(decay_sum)[:, None, None] * state + added, state)


def pick_group(values, group):
    shaped = values.reshape(values.shape[:-1] + (N, G))
    return lax.dynamic_index_in_dim(shaped, group, shaped.ndim - 1, keepdims=False)


def on_device(
    tokens,
    project_weight,
    state_weight,
    step_weight,
    mixer_taps,
    state_taps,
    step_bias,
    decay_log,
    norm_gain,
):
    inner_id = lax.axis_index("inner")
    project_rows, state_rows, step_rows = (
        lax.all_gather(project_weight, "ctx", axis=0, tiled=True),
        lax.all_gather(state_weight, "ctx", axis=0, tiled=True),
        lax.all_gather(step_weight, "ctx", axis=0, tiled=True),
    )
    heads_here = step_weight.shape[1]
    width_here = project_weight.shape[2]
    model_width = project_rows.shape[0]
    group = inner_id * heads_here // (H // G)
    slice_cols = state_weight.shape[2]
    state_conv = lax.dynamic_slice_in_dim(state_taps, inner_id * slice_cols, slice_cols, 2)
    joined = jnp.concatenate(
        [
            project_rows.reshape(model_width, 2 * width_here),
            state_rows.reshape(model_width, 2 * slice_cols),
            step_rows,
        ],
        axis=1,
    )
    projected = jnp.dot(
        lax.all_gather(tokens, "inner", axis=0, tiled=True),
        joined,
        preferred_element_type=jnp.float32,
    ).astype(jnp.bfloat16)
    rows_total = projected.shape[0]
    gate_values = projected[:, :width_here]
    x_pre = projected[:, width_here : 2 * width_here]
    state_pre = projected[:, 2 * width_here : 2 * width_here + 2 * slice_cols].reshape(
        rows_total, 2, slice_cols
    )
    step_raw = projected[:, 2 * width_here + 2 * slice_cols :]
    edge_row = rows_total - (CONV - 1)
    prior_x, prior_state = passed_along((x_pre[edge_row:], state_pre[edge_row:]), "ctx", 1)
    x_vals = conv_apply(mixer_taps, prior_x, x_pre)
    state_vals = conv_apply(state_conv, prior_state, state_pre)
    state_all = lax.all_gather(state_vals, "inner", axis=2, tiled=True)
    state_vals = pick_group(state_all, group)
    blocks = rows_total // SPAN
    b_blocks = state_vals[:, 0].reshape(blocks, SPAN, N)
    c_blocks = state_vals[:, 1].reshape(blocks, SPAN, N)
    step_size = jax.nn.softplus(step_raw.astype(jnp.float32) + step_bias)
    step_heads = step_size.T.reshape(heads_here, blocks, SPAN)
    cumul = jnp.cumsum(step_heads * (-jnp.exp(decay_log))[:, None, None], axis=2)
    scores = jnp.einsum("ctn,csn->cts", c_blocks, b_blocks, preferred_element_type=jnp.float32)
    lower = jnp.tril(jnp.ones((SPAN, SPAN), dtype=bool))
    spacing = jnp.where(lower, cumul[..., :, None] - cumul[..., None, :], -jnp.inf)
    mixing = (scores[None] * jnp.exp(spacing) * step_heads[:, :, None, :]).astype(jnp.bfloat16)
    x_blocks = x_vals.reshape(blocks, SPAN, heads_here, P_SIZE)
    diagonal = jnp.einsum("hcts,cshp->cthp", mixing, x_blocks, preferred_element_type=jnp.float32)
    ending = cumul[:, :, -1]
    to_end = jnp.exp(ending[..., None] - cumul) * step_heads
    weighted_b = (b_blocks.astype(jnp.float32)[None] * to_end[..., None]).astype(jnp.bfloat16)
    fresh = jnp.einsum("hcsn,cshp->chnp", weighted_b, x_blocks, preferred_element_type=jnp.float32)
    empty_state = jnp.zeros((heads_here, N, P_SIZE), jnp.float32)
    block_state, local_in = lax.scan(carry_block, empty_state, (ending.T, fresh))
    block_log = jnp.sum(ending, axis=1)
    before_log = (jnp.cumsum(ending, axis=1) - ending).T
    _, prior_block = entering(
        (block_log, block_state), "ctx", join_chain, (jnp.zeros_like(block_log), empty_state)
    )
    state_in = local_in + jnp.exp(before_log)[:, :, None, None] * prior_block[None]
    c_scaled = (c_blocks.astype(jnp.float32)[None] * jnp.exp(cumul)[..., None]).astype(jnp.bfloat16)
    state_high = state_in.astype(jnp.bfloat16)
    state_low = (state_in - state_high.astype(jnp.float32)).astype(jnp.bfloat16)
    offdiag = jnp.einsum(
        "hctn,chnp->cthp", c_scaled, state_high, preferred_element_type=jnp.float32
    )
    offdiag = offdiag + jnp.einsum(
        "hctn,chnp->cthp", c_scaled, state_low, preferred_element_type=jnp.float32
    )
    outputs = (diagonal + offdiag).reshape(rows_total, width_here)
    gated = (outputs * jax.nn.silu(gate_values.astype(jnp.float32))).astype(jnp.bfloat16)
    gated_wide = gated.astype(jnp.float32)
    squares = jnp.sum(gated_wide * gated_wide, axis=1)
    group_devices = H // G // heads_here
    for bit in range(group_devices.bit_length() - 1):
        squares = squares + partner(squares, "inner", bit)
    power = squares[:, None] / (H * P_SIZE // G)
    gain_here = lax.dynamic_slice_in_dim(norm_gain, inner_id * width_here, width_here, 0)
    normed = (gated_wide * lax.rsqrt(power + EPSILON) * gain_here).astype(jnp.bfloat16)
    result = lax.all_to_all(normed, "inner", split_axis=0, concat_axis=1, tiled=True)
    return result


def solution(mesh):
    placed = (
        P(("ctx", "inner"), None),
        P("ctx", None, "inner"),
        P("ctx", None, "inner"),
        P("ctx", "inner"),
        P(None, "inner"),
        P(),
        P("inner"),
        P("inner"),
        P(),
    )
    return jax.shard_map(
        on_device, mesh=mesh, in_specs=placed, out_specs=P(("ctx", "inner"), None), check_vma=False
    )
```

profile of v0, /device:TPU:25, one launch (start us, length us, event | category | flops | bytes accessed | tf_op | source)
XLA Modules:
  0.0 290.0 jit_solution(8972189394626062334)
XLA Ops:
  8.8 14.7 %all_gather.27 = bf16[2048,16]{0,1:T(8,128)(2,1)S(1)} all-gather(bf16[256,16]{0,1:T(8,128)(2,1)} %param.16), channel_id=1, replica_groups=mesh['ctx'=8,'inner'=4] {'ctx'}, dimensions={0}, use_global_device_ids=true | all-gather | bytes 73728 | tf_op jit(solution)/shard_map/all_gather | solution.py:85
  23.5 1.0 copy.91
  24.5 6.7 %all-gather.10.cloned.1.call-done = bf16[2048,2,128]{2,1,0:T(2,128)(2,1)} async-done(((bf16[256,2,128]{2,1,0:T(2,128)(2,1)}), bf16[2048,2,128]{2,1,0:T(2,128)(2,1)}) %all-gather.10.cloned.1.call-update) | async-done | bytes 1048592 | tf_op jit(solution)/shard_map/all_gather | solution.py:84
  31.2 1.4 copy.137
  32.6 80.6 %all-gather.8.cloned.1.call-done = bf16[2048,2,1024]{2,1,0:T(2,128)(2,1)} async-done(((bf16[256,2,1024]{2,1,0:T(2,128)(2,1)}), bf16[2048,2,1024]{2,1,0:T(2,128)(2,1)}) %all-gather.8.cloned.1.call-update) | async-done | bytes 8388624 | tf_op jit(solution)/shard_map/all_gather | solution.py:83
  113.2 10.2 %copy.119 = bf16[256,8,2,1024]{3,1,2,0:T(8,128)(2,1)} copy(bf16[256,8,2,1024]{3,2,1,0:T(2,128)(2,1)} %bitcast.91) | data formatting | bytes 16777216
  123.3 27.6 %all-gather.12.cloned.1.call-done = bf16[512,2048]{1,0:T(8,128)(2,1)} async-done(((bf16[128,2048]{1,0:T(8,128)(2,1)}), bf16[512,2048]{1,0:T(8,128)(2,1)}) %all-gather.12.cloned.1.call-update) | async-done | bytes 2097168 | tf_op jit(solution)/shard_map/all_gather | solution.py:102
  150.9 9.8 %fusion.11 = bf16[512,2320]{0,1:T(8,128)(2,1)S(1)} fusion(bf16[512,2048]{1,0:T(8,128)(2,1)} %all-gather.12.cloned.1.call-done, bf16[2048,16]{1,0:T(8,128)(2,1)} %copy.91, bf16[2048,256]{1,0:T(8,128)(2,1)S(1)} %bitcast.100, bf16[2048,2048]{1,0:T(8,128)(2,1)} %bitcast.92), kind=kOutput, calls=%fused_computation.20 | convolution fusion | flops 4895088640 | bytes 13975552 | tf_op jit(solution)/shard_map/dot_general | solution.py:101
  161.0 1.3 collective-permute-start.1
  163.7 1.8 copy.94
  165.5 2.5 multiply_convert_fusion.10
  168.0 1.8 copy.96
  170.0 0.8 slice.106
  170.8 1.5 collective-permute-start
  172.4 1.2 reduce_window_sum.22
  174.0 1.6 collective-permute-done
  175.5 3.8 %multiply_convert_fusion.7 = bf16[512,1024]{0,1:T(8,128)(2,1)S(1)} fusion(bf16[512,1024]{0,1:T(8,128)(2,1)S(1)} %slice.107, bf16[3,1024]{0,1:T(8,128)(2,1)} %collective-permute-done, f32[1024]{0:T(1024)S(1)} %bitcast.112, f32[1024]{0:T(1024)S(1)} %bitcast.113, f32[1024]{0:T(1024)S(1)} %bitcast.110, f32[1024]{0:T(1024)S(1)} %bitcast.111, f32[1024]{0:T(1024)S(1)} %bitcast.109), kind=kLoop, calls=%fused_computation.53 | loop fusion | flops 13631488 | bytes 2123776 | tf_op jit(solution)/shard_map/convert_element_type | solution.py:53
  179.6 17.8 %all-gather.14.cloned.1.call-done = bf16[512,2,512]{0,1,2:T(2,128)(2,1)} async-done(((bf16[512,2,128]{0,1,2:T(2,128)(2,1)}), bf16[512,2,512]{0,1,2:T(2,128)(2,1)}) %all-gather.14.cloned.1.call-update) | async-done | bytes 1048592 | tf_op jit(solution)/shard_map/all_gather | solution.py:117
  197.4 1.1 constant_dynamic-slice_fusion.6
  198.9 4.0 %fusion.26 = f32[4,16,128,64]{3,2,1,0:T(8,128)} fusion(f32[16,4,128]{2,0,1:T(8,128)S(1)} %get-tuple-element.170, f32[4,128,128]{2,1,0:T(8,128)S(1)} %convert_element_type.129, bf16[4,128,16,64]{1,0,3,2:T(4,128)(2,1)S(1)} %reshape.90), kind=kOutput, calls=%fused_computation.36 | convolution fusion | flops 136314880 | bytes 3440640 | tf_op jit(solution)/shard_map/hcsn,cshp->chnp/dot_general | solution.py:134
  202.8 10.1 %while.26 = (s32[]{:T(128)}, f32[16,128,64]{2,1,0:T(8,128)S(1)}, f32[4,16,128,64]{3,2,1,0:T(8,128)}, f32[4,16]{1,0:T(4,128)S(1)}, f32[4,16,128,64]{3,2,1,0:T(8,128)}, /*index=5*/s32[]{:T(128)}, s32[]{:T(128)}) while((s32[]{:T(128)}, f32[16,128,64]{2,1,0:T(8,128)S(1)}, f32[4,16,128,64]{3,2,1,0:T(8,128)}, f32[4,16]{1,0:T(4,128)S(1)}, ...), condition=%wide.region_2.3_spmd.clone, body=%wide.region_1.2_spmd.clone.sunk | while | flops 524291 | bytes 3146528 | solution.py:136
  202.8 1.1 bitcast_dynamic-update-slice_fusion.2
  203.9 1.4 bitcast_add_fusion.2
  205.3 1.1 bitcast_dynamic-update-slice_fusion.2
  206.4 1.4 bitcast_add_fusion.2
  207.9 1.1 bitcast_dynamic-update-slice_fusion.2
  209.0 1.4 bitcast_add_fusion.2
  210.4 1.1 bitcast_dynamic-update-slice_fusion.2
  211.5 1.4 bitcast_add_fusion.2
  213.0 0.9 copy.104
  215.4 13.6 %all-reduce = bf16[128]{0:T(256)(128)(2,1)S(1)} all-reduce(bf16[128]{0:T(256)(128)(2,1)S(1)} %dynamic-update-slice), channel_id=2, replica_groups=mesh['ctx'=8,'inner'=4] {'ctx'}, use_global_device_ids=true, to_apply=%add | all-reduce | flops 128 | bytes 512
  229.2 0.8 copy_bitcast_fusion.2
  230.2 3.3 %fusion.18 = f32[4,16,64,128]{3,2,1,0:T(8,128)} fusion(f32[16,4,128]{2,0,1:T(8,128)S(1)} %copy_bitcast_fusion.2, f32[16,4,128]{2,0,1:T(8,128)S(1)} %reduce_window_sum.22, f32[4,128,128]{2,1,0:T(8,128)S(1)} %fusion.65, pred[128,128]{1,0:T(8,128)(4,1)S(1)} %iota_compare_fusion, bf16[4,128,16,64]{1,0,3,2:T(4,128)(2,1)S(1)} %reshape.90), kind=kOutput, calls=%fused_computation.28 | convolution fusion | flops 139460608 | bytes 3489792 | tf_op jit(solution)/shard_map/hcts,cshp->cthp/dot_general | solution.py:130
  233.6 8.9 %all-gather.16.cloned.1.call-done = bf16[128,128,64]{1,2,0:T(8,128)(2,1)} async-done(((bf16[16,128,64]{1,2,0:T(8,128)(2,1)}), bf16[128,128,64]{1,2,0:T(8,128)(2,1)}) %all-gather.16.cloned.1.call-update) | async-done | bytes 2097168 | tf_op jit(solution)/shard_map/all_gather | solution.py:24
  242.5 11.0 %while.25 = (s32[]{:T(128)}, f32[16,128,64]{2,1,0:T(8,128)S(1)}, s32[]{:T(128)}, bf16[8,16]{1,0:T(8,128)(2,1)S(1)}, bf16[8,16,128,64]{2,3,1,0:T(8,128)(2,1)}, /*index=5*/s32[]{:T(128)}, s32[]{:T(128)}, s32[]{:T(128)}) while((s32[]{:T(128)}, f32[16,128,64]{2,1,0:T(8,128)S(1)}, s32[]{:T(128)}, bf16[8,16]{1,0:T(8,128)(2,1)S(1)}, ...), condition=%wide.region_6.7_spmd, body=%wide.region_5.6_spmd.sunk | while | flops 393237 | bytes 2359583 | solution.py:38
  242.6 1.0 constant_dynamic-slice_fusion.9
  244.1 1.0 constant_dynamic-slice_fusion.9
  245.7 1.0 constant_dynamic-slice_fusion.9
  247.3 1.0 constant_dynamic-slice_fusion.9
  248.8 1.0 constant_dynamic-slice_fusion.9
  250.4 1.0 constant_dynamic-slice_fusion.9
  252.0 1.0 constant_dynamic-slice_fusion.9
  253.5 5.2 %fusion.15 = f32[4,16,64,128]{3,2,1,0:T(8,128)S(1)} fusion(f32[4,16,128,64]{3,2,1,0:T(8,128)} %get-tuple-element.77, f32[16,4,128]{2,0,1:T(8,128)S(1)} %get-tuple-element.169, f32[4,128,128]{2,1,0:T(8,128)S(1)} %convert_element_type.135, f32[16,128,64]{2,1,0:T(8,128)S(1)} %get-tuple-element.79, f32[4,16]{1,0:T(4,128)S(1)} %exponential_bitcast_fusion.1), kind=kOutput, calls=%fused_computation.22 | convolution fusion | flops 139460608 | bytes 5013760 | tf_op jit(solution)/shard_map/hctn,chnp->cthp/dot_general | solution.py:149
  258.8 2.7 add_bitcast_fusion
  261.5 1.4 copy.108
  262.9 2.0 fusion.23
  265.3 16.9 %all_to_all.19 = bf16[4,128,1024]{1,2,0:T(8,128)(2,1)S(1)} all-to-all(bf16[4,128,1024]{1,2,0:T(8,128)(2,1)S(1)} %copy_bitcast_fusion.1), channel_id=1, replica_groups=mesh['ctx'=8,'inner'=4] {'inner'}, dimensions={0} | all-to-all | bytes 2097152 | tf_op jit(solution)/shard_map/all_to_all | solution.py:162
  282.2 1.3 copy.110
  (80 shorter events, 10.5 us)
Async XLA Ops:
  6.5 24.7 %all-gather.10.cloned.1.call-start = ((), (), s32[]{:S(2)}) async-start(), calls=%async_computation.2 | async-start | bytes 1179648 | tf_op jit(solution)/shard_map/all_gather | solution.py:84
  7.3 105.9 %all-gather.8.cloned.1.call-start = ((), (), s32[]{:S(2)}) async-start(), calls=%async_computation.1 | async-start | bytes 9437184 | tf_op jit(solution)/shard_map/all_gather | solution.py:83
  8.0 142.9 %all-gather.12.cloned.1.call-start = ((), (), s32[]{:S(2)}) async-start(), calls=%async_computation.3 | async-start | bytes 2621440 | tf_op jit(solution)/shard_map/all_gather | solution.py:102
  8.7 188.7 %all-gather.14.cloned.1.call-start = ((), (), s32[]{:S(2)}) async-start(), calls=%async_computation.4 | async-start | bytes 1310720 | tf_op jit(solution)/shard_map/all_gather | solution.py:117
  160.7 13.2 %copy-start.1 = (bf16[512,2320]{0,1:T(8,128)(2,1)}, bf16[512,2320]{0,1:T(8,128)(2,1)S(1)}, u32[]{:S(2)}) copy-start(bf16[512,2320]{0,1:T(8,128)(2,1)S(1)} %fusion.11) | copy-start | bytes 7127044
  160.7 9.2 %copy-start.5 = (f32[16]{0:T(128)S(1)}, f32[16]{0:T(128)}, u32[]{:S(2)}) copy-start(f32[16]{0:T(128)} %param.20) | copy-start | bytes 196
  160.8 9.2 %copy-start.3 = (f32[5,1024]{1,0:T(8,128)S(1)}, f32[5,1024]{1,0:T(8,128)}, u32[]{:S(2)}) copy-start(f32[5,1024]{1,0:T(8,128)} %param.17) | copy-start | bytes 61444
  160.8 11.5 %copy-start.4 = (f32[16]{0:T(128)S(1)}, f32[16]{0:T(128)}, u32[]{:S(2)}) copy-start(f32[16]{0:T(128)} %param.19) | copy-start | bytes 196
  161.0 4.6 %collective-permute-start.1 = (bf16[3,2,128]{2,0,1:T(4,128)(2,1)S(1)}, bf16[3,2,128]{2,0,1:T(4,128)(2,1)S(1)}, u32[]{:S(2)}, u32[]{:S(2)}) collective-permute-start(bf16[3,2,128]{2,0,1:T(4,128)(2,1)S(1)} %copy.93), channel_id=1, source_target_pairs={{0,4},{4,8},{8,12},{12,16},{16,20},{20,24},{24,28},{1,5},{5,9},{9,... | collective-permute-start | bytes 4616 | tf_op jit(solution)/shard_map/ppermute | solution.py:18
  169.9 72.6 %all-gather.16.cloned.1.call-start = ((), (), s32[]{:S(2)}) async-start(), calls=%async_computation.5 | async-start | bytes 2359296 | tf_op jit(solution)/shard_map/all_gather | solution.py:24
  170.8 4.7 %collective-permute-start = (bf16[3,1024]{0,1:T(8,128)(2,1)}, bf16[3,1024]{0,1:T(8,128)(2,1)}, u32[]{:S(2)}, u32[]{:S(2)}) collective-permute-start(bf16[3,1024]{0,1:T(8,128)(2,1)} %slice.106), channel_id=1, source_target_pairs={{0,4},{4,8},{8,12},{12,16},{16,20},{20,24},{24,28},{1,5},{5,9},{9,... | collective-permute-start | bytes 18440 | tf_op jit(solution)/shard_map/ppermute | solution.py:18
  202.8 11.1 %copy-start.6 = (u32[32]{0:T(128)S(1)}, u32[32]{0:T(128)}, u32[]{:S(2)}) copy-start(u32[32]{0:T(128)} %constant.96) | copy-start | bytes 388
  253.5 5.3 %copy-start = (f32[4,16,128,64]{3,2,1,0:T(8,128)S(1)}, f32[4,16,128,64]{3,2,1,0:T(8,128)}, u32[]{:S(2)}) copy-start(f32[4,16,128,64]{3,2,1,0:T(8,128)} %get-tuple-element.77) | copy-start | bytes 6291460
  253.5 5.3 %copy-start.2 = (f32[4,16,64,128]{3,2,1,0:T(8,128)S(1)}, f32[4,16,64,128]{3,2,1,0:T(8,128)}, u32[]{:S(2)}) copy-start(f32[4,16,64,128]{3,2,1,0:T(8,128)} %fusion.18) | copy-start | bytes 6291460
  262.9 2.0 dynamic-slice-start
Sparse Core Ops, SparseCore 0:
  8.9 22.2 all-gather.9
  32.8 80.3 all-gather.7
  115.0 35.8 all-gather.11
  170.0 27.4 all-gather.13
  214.0 28.3 all-gather.15
where the time goes:
time: 291 us; the launch traced here: 290 us
  waiting for transfers between devices  145 us (50%)
  blocking collectives  45.3 us (16%)
  local copies, waits for them, and re-layouts  33.9 us (12%)
  matrix products  25.2 us (9%)
  other arithmetic  22.9 us (8%)
  between operations  14.1 us (5%)
  starting transfers between devices  2.92 us (1%)
    all_gather x1, waiting for transfers between devices, on_device(): lax.all_gather(project_weight, 'ctx', axis=0, tiled=True)  80.6 us
    all_gather x1, waiting for transfers between devices, on_device(): lax.all_gather(tokens, 'inner', axis=0, tiled=True)  27.6 us
    all_gather x1, waiting for transfers between devices, on_device(): state_all = lax.all_gather(state_vals, 'inner', axis=2, tiled=True)  17.8 us
    all_to_all x1, blocking collectives, on_device(): lax.all_to_all(normed, 'inner', split_axis=0, concat_axis=1, tiled=True)  16.9 us
    all_gather x1, blocking collectives, on_device(): lax.all_gather(step_weight, 'ctx', axis=0, tiled=True)  14.7 us
    unnamed x1, blocking collectives  13.6 us
    unnamed x19, local copies, waits for them, and re-layouts  12.4 us
    dot_general x1, matrix products, on_device(): jnp.dot(lax.all_gather(tokens, 'inner', axis=0, tiled=True), joined, pref...  9.82 us
  transfers between devices with their start and end apart: 7, of which 6 were waited for; matrix products, arithmetic and copies ran while one was open for 10% of the time, Pallas kernels for 0%

commit v1 on v0

--- a/solution.py
+++ b/solution.py
@@ -10,6 +10,11 @@
 CONV = 4
 SPAN = 128
 EPSILON = 1e-05
+
+
+def prepare_strings(patch, along_axis):
+    y2 = lax.all_gather(patch, along_axis)
+    return jnp.concatenate(y2, axis=2)
 
 
 def passed_along(x, axis, by):
@@ -114,7 +119,7 @@
     prior_x, prior_state = passed_along((x_pre[edge_row:], state_pre[edge_row:]), "ctx", 1)
     x_vals = conv_apply(mixer_taps, prior_x, x_pre)
     state_vals = conv_apply(state_conv, prior_state, state_pre)
-    state_all = lax.all_gather(state_vals, "inner", axis=2, tiled=True)
+    state_all = prepare_strings(state_vals, "inner")
     state_vals = pick_group(state_all, group)
     blocks = rows_total // SPAN
     b_blocks = state_vals[:, 0].reshape(blocks, SPAN, N)

time: 291 us -> 291 us (level)
  no operation moved by 1% of the time
where the time goes in v1:
time: 291 us; the launch traced here: 290 us
  waiting for transfers between devices  145 us (50%)
  blocking collectives  45.3 us (16%)
  local copies, waits for them, and re-layouts  33.6 us (12%)
  matrix products  25.2 us (9%)
  other arithmetic  22.9 us (8%)
  between operations  14.1 us (5%)
  starting transfers between devices  2.92 us (1%)
    all_gather x1, waiting for transfers between devices, on_device(): lax.all_gather(project_weight, 'ctx', axis=0, tiled=True)  80.6 us
    all_gather x1, waiting for transfers between devices, on_device(): lax.all_gather(tokens, 'inner', axis=0, tiled=True)  27.6 us
    all_gather x1, waiting for transfers between devices, prepare_strings(): y2 = lax.all_gather(patch, along_axis)  17.8 us
    all_to_all x1, blocking collectives, on_device(): lax.all_to_all(normed, 'inner', split_axis=0, concat_axis=1, tiled=True)  16.9 us
    all_gather x1, blocking collectives, on_device(): lax.all_gather(step_weight, 'ctx', axis=0, tiled=True)  14.7 us
    unnamed x1, blocking collectives  13.7 us
    unnamed x19, local copies, waits for them, and re-layouts  12.4 us
    dot_general x1, matrix products, on_device(): jnp.dot(lax.all_gather(tokens, 'inner', axis=0, tiled=True), joined, pref...  9.82 us
  transfers between devices with their start and end apart: 7, of which 6 were waited for; matrix products, arithmetic and copies ran while one was open for 10% of the time, Pallas kernels for 0%

profile of v1, /device:TPU:25, one launch (start us, length us, event | category | flops | bytes accessed | tf_op | source)
XLA Modules:
  0.0 289.8 jit_solution(12553801805903941235)
XLA Ops:
  8.8 14.7 %all_gather.30 = bf16[2048,16]{0,1:T(8,128)(2,1)S(1)} all-gather(bf16[256,16]{0,1:T(8,128)(2,1)} %param.16), channel_id=1, replica_groups=mesh['ctx'=8,'inner'=4] {'ctx'}, dimensions={0}, use_global_device_ids=true | all-gather | bytes 73728 | tf_op jit(solution)/shard_map/all_gather | solution.py:90
  23.5 1.0 copy.63
  24.5 6.7 %all-gather.11.cloned.1.call-done = bf16[2048,2,128]{2,1,0:T(2,128)(2,1)} async-done(((bf16[256,2,128]{2,1,0:T(2,128)(2,1)}), bf16[2048,2,128]{2,1,0:T(2,128)(2,1)}) %all-gather.11.cloned.1.call-update) | async-done | bytes 1048592 | tf_op jit(solution)/shard_map/all_gather | solution.py:89
  31.2 1.4 copy.106
  32.6 80.6 %all-gather.9.cloned.1.call-done = bf16[2048,2,1024]{2,1,0:T(2,128)(2,1)} async-done(((bf16[256,2,1024]{2,1,0:T(2,128)(2,1)}), bf16[2048,2,1024]{2,1,0:T(2,128)(2,1)}) %all-gather.9.cloned.1.call-update) | async-done | bytes 8388624 | tf_op jit(solution)/shard_map/all_gather | solution.py:88
  113.2 10.2 %copy.88 = bf16[256,8,2,1024]{3,1,2,0:T(8,128)(2,1)} copy(bf16[256,8,2,1024]{3,2,1,0:T(2,128)(2,1)} %bitcast.94) | data formatting | bytes 16777216
  123.3 27.6 %all-gather.13.cloned.1.call-done = bf16[512,2048]{1,0:T(8,128)(2,1)} async-done(((bf16[128,2048]{1,0:T(8,128)(2,1)}), bf16[512,2048]{1,0:T(8,128)(2,1)}) %all-gather.13.cloned.1.call-update) | async-done | bytes 2097168 | tf_op jit(solution)/shard_map/all_gather | solution.py:107
  150.9 9.8 %fusion.11 = bf16[512,2320]{0,1:T(8,128)(2,1)S(1)} fusion(bf16[512,2048]{1,0:T(8,128)(2,1)} %all-gather.13.cloned.1.call-done, bf16[2048,16]{1,0:T(8,128)(2,1)} %copy.63, bf16[2048,256]{1,0:T(8,128)(2,1)S(1)} %bitcast.105, bf16[2048,2048]{1,0:T(8,128)(2,1)} %bitcast.95), kind=kOutput, calls=%fused_computation.20 | convolution fusion | flops 4895088640 | bytes 13975552 | tf_op jit(solution)/shard_map/dot_general | solution.py:106
  161.0 1.3 collective-permute-start.1
  162.3 0.8 fusion.55
  163.7 1.8 copy.65
  165.5 2.5 multiply_convert_fusion.10
  168.1 0.9 slice.106
  169.0 1.5 collective-permute-start
  170.6 1.2 reduce_window_sum.22
  172.1 1.6 collective-permute-done
  173.7 3.8 %multiply_convert_fusion.7 = bf16[512,1024]{0,1:T(8,128)(2,1)S(1)} fusion(bf16[512,1024]{0,1:T(8,128)(2,1)S(1)} %slice.107, bf16[3,1024]{0,1:T(8,128)(2,1)} %collective-permute-done, f32[1024]{0:T(1024)S(1)} %bitcast.116, f32[1024]{0:T(1024)S(1)} %bitcast.117, f32[1024]{0:T(1024)S(1)} %bitcast.114, f32[1024]{0:T(1024)S(1)} %bitcast.115, f32[1024]{0:T(1024)S(1)} %bitcast.113), kind=kLoop, calls=%fused_computation.53 | loop fusion | flops 13631488 | bytes 2123776 | tf_op jit(solution)/shard_map/convert_element_type | solution.py:58
  177.8 17.8 %all-gather.15.cloned.1.call-done = bf16[2048,2,128]{2,0,1:T(8,128)(2,1)} async-done(((bf16[512,2,128]{2,0,1:T(8,128)(2,1)}), bf16[2048,2,128]{2,0,1:T(8,128)(2,1)}) %all-gather.15.cloned.1.call-update) | async-done | bytes 1048592 | tf_op jit(solution)/shard_map/all_gather | solution.py:16
  195.6 2.5 copy.67
  198.6 4.0 %fusion.26 = f32[4,16,128,64]{3,2,1,0:T(8,128)} fusion(f32[16,4,128]{2,0,1:T(8,128)S(1)} %get-tuple-element.155, f32[4,128,128]{2,1,0:T(8,128)S(1)} %convert_element_type.129, bf16[4,128,16,64]{1,0,3,2:T(4,128)(2,1)S(1)} %reshape.90), kind=kOutput, calls=%fused_computation.36 | convolution fusion | flops 136314880 | bytes 3440640 | tf_op jit(solution)/shard_map/hcsn,cshp->chnp/dot_general | solution.py:139
  202.6 10.1 %while.26 = (s32[]{:T(128)}, f32[16,128,64]{2,1,0:T(8,128)S(1)}, f32[4,16,128,64]{3,2,1,0:T(8,128)}, f32[4,16]{1,0:T(4,128)S(1)}, f32[4,16,128,64]{3,2,1,0:T(8,128)}, /*index=5*/s32[]{:T(128)}, s32[]{:T(128)}) while((s32[]{:T(128)}, f32[16,128,64]{2,1,0:T(8,128)S(1)}, f32[4,16,128,64]{3,2,1,0:T(8,128)}, f32[4,16]{1,0:T(4,128)S(1)}, ...), condition=%wide.region_2.3_spmd.clone, body=%wide.region_1.2_spmd.clone.sunk | while | flops 524291 | bytes 3146528 | solution.py:141
  202.6 1.1 bitcast_dynamic-update-slice_fusion.2
  203.6 1.4 bitcast_add_fusion.2
  205.1 1.1 bitcast_dynamic-update-slice_fusion.2
  206.2 1.4 bitcast_add_fusion.2
  207.6 1.1 bitcast_dynamic-update-slice_fusion.2
  208.7 1.4 bitcast_add_fusion.2
  210.2 1.1 bitcast_dynamic-update-slice_fusion.2
  211.3 1.4 bitcast_add_fusion.2
  212.7 0.9 copy.75
  215.2 13.7 %all-reduce = bf16[128]{0:T(256)(128)(2,1)S(1)} all-reduce(bf16[128]{0:T(256)(128)(2,1)S(1)} %dynamic-update-slice), channel_id=3, replica_groups=mesh['ctx'=8,'inner'=4] {'ctx'}, use_global_device_ids=true, to_apply=%add | all-reduce | flops 128 | bytes 512
  228.9 0.8 copy_bitcast_fusion.2
  230.0 3.3 %fusion.18 = f32[4,16,64,128]{3,2,1,0:T(8,128)} fusion(f32[16,4,128]{2,0,1:T(8,128)S(1)} %copy_bitcast_fusion.2, f32[16,4,128]{2,0,1:T(8,128)S(1)} %reduce_window_sum.22, f32[4,128,128]{2,1,0:T(8,128)S(1)} %fusion.65, pred[128,128]{1,0:T(8,128)(4,1)S(1)} %iota_compare_fusion, bf16[4,128,16,64]{1,0,3,2:T(4,128)(2,1)S(1)} %reshape.90), kind=kOutput, calls=%fused_computation.28 | convolution fusion | flops 139460608 | bytes 3489792 | tf_op jit(solution)/shard_map/hcts,cshp->cthp/dot_general | solution.py:135
  233.3 8.9 %all-gather.17.cloned.1.call-done = bf16[128,128,64]{1,2,0:T(8,128)(2,1)} async-done(((bf16[16,128,64]{1,2,0:T(8,128)(2,1)}), bf16[128,128,64]{1,2,0:T(8,128)(2,1)}) %all-gather.17.cloned.1.call-update) | async-done | bytes 2097168 | tf_op jit(solution)/shard_map/all_gather | solution.py:29
  242.3 11.0 %while.25 = (s32[]{:T(128)}, f32[16,128,64]{2,1,0:T(8,128)S(1)}, s32[]{:T(128)}, bf16[8,16]{1,0:T(8,128)(2,1)S(1)}, bf16[8,16,128,64]{2,3,1,0:T(8,128)(2,1)}, /*index=5*/s32[]{:T(128)}, s32[]{:T(128)}, s32[]{:T(128)}) while((s32[]{:T(128)}, f32[16,128,64]{2,1,0:T(8,128)S(1)}, s32[]{:T(128)}, bf16[8,16]{1,0:T(8,128)(2,1)S(1)}, ...), condition=%wide.region_6.7_spmd, body=%wide.region_5.6_spmd.sunk | while | flops 393237 | bytes 2359583 | solution.py:43
  242.3 1.0 constant_dynamic-slice_fusion.9
  243.9 1.0 constant_dynamic-slice_fusion.9
  245.5 1.0 constant_dynamic-slice_fusion.9
  247.0 1.0 constant_dynamic-slice_fusion.9
  248.6 1.0 constant_dynamic-slice_fusion.9
  250.1 1.0 constant_dynamic-slice_fusion.9
  251.7 1.0 constant_dynamic-slice_fusion.9
  253.3 5.2 %fusion.15 = f32[4,16,64,128]{3,2,1,0:T(8,128)S(1)} fusion(f32[4,16,128,64]{3,2,1,0:T(8,128)} %get-tuple-element.77, f32[16,4,128]{2,0,1:T(8,128)S(1)} %get-tuple-element.154, f32[4,128,128]{2,1,0:T(8,128)S(1)} %convert_element_type.135, f32[16,128,64]{2,1,0:T(8,128)S(1)} %get-tuple-element.79, f32[4,16]{1,0:T(4,128)S(1)} %exponential_bitcast_fusion.1), kind=kOutput, calls=%fused_computation.22 | convolution fusion | flops 139460608 | bytes 5013760 | tf_op jit(solution)/shard_map/hctn,chnp->cthp/dot_general | solution.py:154
  258.5 2.7 add_bitcast_fusion
  261.2 1.4 copy.79
  262.6 2.0 fusion.23
  265.0 16.9 %all_to_all.19 = bf16[4,128,1024]{1,2,0:T(8,128)(2,1)S(1)} all-to-all(bf16[4,128,1024]{1,2,0:T(8,128)(2,1)S(1)} %copy_bitcast_fusion.1), channel_id=1, replica_groups=mesh['ctx'=8,'inner'=4] {'inner'}, dimensions={0} | all-to-all | bytes 2097152 | tf_op jit(solution)/shard_map/all_to_all | solution.py:167
  281.9 1.3 copy.81
  (80 shorter events, 9.9 us)
Async XLA Ops:
  6.5 24.7 %all-gather.11.cloned.1.call-start = ((), (), s32[]{:S(2)}) async-start(), calls=%async_computation.2 | async-start | bytes 1179648 | tf_op jit(solution)/shard_map/all_gather | solution.py:89
  7.3 105.9 %all-gather.9.cloned.1.call-start = ((), (), s32[]{:S(2)}) async-start(), calls=%async_computation.1 | async-start | bytes 9437184 | tf_op jit(solution)/shard_map/all_gather | solution.py:88
  8.0 142.9 %all-gather.13.cloned.1.call-start = ((), (), s32[]{:S(2)}) async-start(), calls=%async_computation.3 | async-start | bytes 2621440 | tf_op jit(solution)/shard_map/all_gather | solution.py:107
  8.7 186.9 %all-gather.15.cloned.1.call-start = ((), (), s32[]{:S(2)}) async-start(), calls=%async_computation.4 | async-start | bytes 1310720 | tf_op jit(solution)/shard_map/all_gather | solution.py:16
  160.7 11.4 %copy-start.1 = (bf16[512,2320]{0,1:T(8,128)(2,1)}, bf16[512,2320]{0,1:T(8,128)(2,1)S(1)}, u32[]{:S(2)}) copy-start(bf16[512,2320]{0,1:T(8,128)(2,1)S(1)} %fusion.11) | copy-start | bytes 7127044
  160.7 7.3 %copy-start.5 = (f32[16]{0:T(128)S(1)}, f32[16]{0:T(128)}, u32[]{:S(2)}) copy-start(f32[16]{0:T(128)} %param.20) | copy-start | bytes 196
  160.8 7.3 %copy-start.3 = (f32[5,1024]{1,0:T(8,128)S(1)}, f32[5,1024]{1,0:T(8,128)}, u32[]{:S(2)}) copy-start(f32[5,1024]{1,0:T(8,128)} %param.17) | copy-start | bytes 61444
  160.8 9.7 %copy-start.4 = (f32[16]{0:T(128)S(1)}, f32[16]{0:T(128)}, u32[]{:S(2)}) copy-start(f32[16]{0:T(128)} %param.19) | copy-start | bytes 196
  161.0 4.6 %collective-permute-start.1 = (bf16[3,2,128]{2,0,1:T(4,128)(2,1)S(1)}, bf16[3,2,128]{2,0,1:T(4,128)(2,1)S(1)}, u32[]{:S(2)}, u32[]{:S(2)}) collective-permute-start(bf16[3,2,128]{2,0,1:T(4,128)(2,1)S(1)} %copy.64), channel_id=1, source_target_pairs={{0,4},{4,8},{8,12},{12,16},{16,20},{20,24},{24,28},{1,5},{5,9},{9,... | collective-permute-start | bytes 4616 | tf_op jit(solution)/shard_map/ppermute | solution.py:23
  168.0 74.2 %all-gather.17.cloned.1.call-start = ((), (), s32[]{:S(2)}) async-start(), calls=%async_computation.5 | async-start | bytes 2359296 | tf_op jit(solution)/shard_map/all_gather | solution.py:29
  169.0 4.7 %collective-permute-start = (bf16[3,1024]{0,1:T(8,128)(2,1)}, bf16[3,1024]{0,1:T(8,128)(2,1)}, u32[]{:S(2)}, u32[]{:S(2)}) collective-permute-start(bf16[3,1024]{0,1:T(8,128)(2,1)} %slice.106), channel_id=1, source_target_pairs={{0,4},{4,8},{8,12},{12,16},{16,20},{20,24},{24,28},{1,5},{5,9},{9,... | collective-permute-start | bytes 18440 | tf_op jit(solution)/shard_map/ppermute | solution.py:23
  202.6 11.1 %copy-start.6 = (u32[32]{0:T(128)S(1)}, u32[32]{0:T(128)}, u32[]{:S(2)}) copy-start(u32[32]{0:T(128)} %constant.96) | copy-start | bytes 388
  253.3 5.3 %copy-start = (f32[4,16,128,64]{3,2,1,0:T(8,128)S(1)}, f32[4,16,128,64]{3,2,1,0:T(8,128)}, u32[]{:S(2)}) copy-start(f32[4,16,128,64]{3,2,1,0:T(8,128)} %get-tuple-element.77) | copy-start | bytes 6291460
  253.3 5.3 %copy-start.2 = (f32[4,16,64,128]{3,2,1,0:T(8,128)S(1)}, f32[4,16,64,128]{3,2,1,0:T(8,128)}, u32[]{:S(2)}) copy-start(f32[4,16,64,128]{3,2,1,0:T(8,128)} %fusion.18) | copy-start | bytes 6291460
  262.6 2.0 dynamic-slice-start
Sparse Core Ops, SparseCore 0:
  8.9 22.2 all-gather.10
  32.8 80.3 all-gather.8
  115.0 35.8 all-gather.12
  168.1 27.4 all-gather.14
  213.8 28.3 all-gather.16
